TPU v7x, 32 devices: a whole 2x2x4 slice. The times are simulated.
32 devices in a mesh: grp: 2 (over x), node: 8 (over z, y), tm: 2 (over core).
Axes of the slice: x: 2, y: 2, z: 4, core: 2. Of those that a mesh axis runs over, the one named last changes fastest.
Arguments:
- scaled_kelvin: float32 [128, 8192], P(('grp', 'node', 'tm')), parts along dimension 0, may hold values from 0.5 to 1.5
- surface_emittance: float32 [16384], P('grp'), parts along dimension 0, may hold values from 0.2 to 1
- loss_factors: float32 [128, 8192], P(('grp', 'node', 'tm')), parts along dimension 0, may hold values from -6 to 6
- gebhart_tiles: bfloat16 [128, 32, 128, 128], P(('grp', 'node')), parts along dimension 0, may hold values from 1.4603138e-06 to 0.0014648438
- tile_target_index: int32 [128, 32], P(('grp', 'node')), parts along dimension 0, may hold values from 0 to 63
- tile_slots_occupied: int32 [128], P(('grp', 'node')), parts along dimension 0, may hold values from 16 to 32, as said below
Outputs:
- temp_sensitivity: float32 [128, 8192], P(('grp', 'node', 'tm')), parts along dimension 0
There are 2 independent parts, one for each index of `grp`. A program takes and returns all parts, laid end to end along the dimension named above; each array names one. Nothing has to cross between parts.
Inputs may be any that keep to these rules, and one draw needn't show every extreme that they name: A row's slots k below tile_slots_occupied are used, the others are ignored; some row of every variant uses all 32.
All inputs are finite; a program needn't handle non-finite values.
Results may differ from a plain program's by a relative error of at most 0.0036.
Values may be sent and summed in bfloat16 or wider, within the bound.
No kernel may reach another device: no remote copies, remote signals or barrier semaphores. Data moves between devices by JAX's collectives and lax.ppermute only.
A program may use at most 192 MiB of HBM per device.

v0:
```python
import jax
import jax.numpy as jnp
from jax import lax
from jax.sharding import PartitionSpec as P


def slot_window(gebhart_tiles, tile_target_index, tile_slots_occupied, slot_start, slot_width):
    in_use = (slot_start + jnp.arange(slot_width, dtype=jnp.int32))[None, :] < tile_slots_occupied[
        :, None
    ]
    return (gebhart_tiles, tile_target_index, in_use)


def over_slots(update, initial, slot_total):
    return update(initial, 0, slot_total)


def on_device(
    scaled_kelvin,
    surface_emittance,
    loss_factors,
    gebhart_tiles,
    tile_target_index,
    tile_slots_occupied,
):
    row_blocks, slot_total, block_side = (
        gebhart_tiles.shape[0],
        gebhart_tiles.shape[1],
        gebhart_tiles.shape[2],
    )
    surface_range = scaled_kelvin.shape[1]
    blocks_all = surface_range // block_side
    own_width = row_blocks * block_side
    own_start = lax.axis_index("node") * own_width
    radiant_output = (surface_emittance[None, :] * scaled_kelvin**4).astype(jnp.bfloat16)
    weights_here = lax.all_to_all(loss_factors, "node", split_axis=1, concat_axis=0, tiled=True)
    panel_rows = lax.all_gather(radiant_output, "node", axis=0, tiled=True)
    row_count = panel_rows.shape[0]
    panel_view = panel_rows.reshape(row_count, blocks_all, block_side)

    def update(running, slot_start, slot_width):
        tiles, columns, in_use = slot_window(
            gebhart_tiles, tile_target_index, tile_slots_occupied, slot_start, slot_width
        )
        picked = jnp.take(panel_view, columns.reshape(-1), axis=1)
        picked = picked.reshape(row_count, row_blocks, slot_width, block_side)
        picked = picked * in_use[None, :, :, None].astype(jnp.bfloat16)
        return jnp.einsum("nrkj,rkij->rni", picked, tiles, preferred_element_type=jnp.float32)

    flux = over_slots(
        update, jnp.zeros((row_blocks, row_count, block_side), jnp.float32), slot_total
    )
    flux = flux.transpose(1, 0, 2).reshape(row_count, own_width)
    own_emit = lax.dynamic_slice_in_dim(panel_rows, own_start, own_width, 1).astype(jnp.float32)
    weight_part = weights_here
    weight = weight_part * (flux - own_emit)
    sample_total = weight.shape[0]
    weight_rows = (
        weight.astype(jnp.bfloat16).reshape(sample_total, row_blocks, block_side).transpose(1, 0, 2)
    )
    weight_part = weight_rows

    def update(running, slot_start, slot_width):
        tiles, columns, in_use = slot_window(
            gebhart_tiles, tile_target_index, tile_slots_occupied, slot_start, slot_width
        )
        contrib = jnp.einsum(
            "rni,rkij->nrkj", weight_part, tiles, preferred_element_type=jnp.float32
        )
        targets = jnp.where(in_use, columns, blocks_all).reshape(-1)
        contrib = contrib.reshape(sample_total, row_blocks * slot_width, block_side)
        return running.at[:, targets, :].add(contrib, mode="drop")

    collected = over_slots(
        update, jnp.zeros((sample_total, blocks_all, block_side), jnp.float32), slot_total
    )
    summed = (
        lax.psum_scatter(
            collected.reshape(sample_total, surface_range).astype(jnp.bfloat16),
            "node",
            scatter_dimension=1,
            tiled=True,
        ).astype(jnp.float32)
        - weight
    )
    costate_vector = lax.all_to_all(summed, "node", split_axis=0, concat_axis=1, tiled=True)
    return 4.0 * surface_emittance[None, :] * scaled_kelvin**3 * costate_vector


def solution(mesh):
    placed = (
        P(("grp", "node", "tm"), None),
        P("grp"),
        P(("grp", "node", "tm"), None),
        P(("grp", "node"), None, None, None),
        P(("grp", "node"), None),
        P(("grp", "node")),
    )
    return jax.shard_map(
        on_device,
        mesh=mesh,
        in_specs=placed,
        out_specs=P(("grp", "node", "tm"), None),
        check_vma=False,
    )
```

profile of v0, /device:TPU:0, one launch (start us, length us, event | category | flops | bytes accessed | tf_op | source)
XLA Modules:
  0.0 169.4 jit_solution(2546197744501569730)
XLA Ops:
  6.5 7.3 %all-to-all-start = ((f32[4,8,1024]{2,0,1:T(4,128)}), f32[4,8,1024]{2,0,1:T(4,128)S(1)}, u32[]{:S(2)}, u32[]{:S(2)}) async-start(f32[4,8,1024]{2,0,1:T(4,128)} %bitcast.50), calls=%async_computation | async-start | bytes 262144 | tf_op jit(solution)/shard_map/all_to_all | solution.py:36
  13.8 0.0 reduce-scatter.2.cloned.1.call-start
  13.9 0.9 fusion.14
  14.8 31.9 %all-gather = bf16[8,4,8192]{2,1,0:T(4,128)(2,1)S(1)} all-gather(bf16[1,4,8192]{2,1,0:T(4,128)(2,1)S(1)} %fusion.14), channel_id=1, replica_groups=mesh['grp'=2,'node'=8,'tm'=2] {'node'}, dimensions={0}, use_global_device_ids=true | all-gather | bytes 589824 | tf_op jit(solution)/shard_map/all_gather | solution.py:37
  46.7 0.5 reshape.117
  47.3 0.3 copy.19
  47.6 0.8 reshape.118
  48.4 0.8 fusion.17
  49.2 1.0 gather_fusion
  50.2 5.2 %fusion.4 = f32[8,4,8,128]{3,2,1,0:T(8,128)S(1)} fusion(bf16[8,32,128,128]{3,2,1,0:T(8,128)(2,1)} %param.9, bf16[32,8,32,128]{3,0,2,1:T(8,128)(2,1)S(1)} %bitcast.46, pred[8,32]{1,0:T(8,128)(4,1)S(1)} %get-tuple-element.6, bf16[8,32]{1,0:T(8,128)(2,1)S(1)} %get-tuple-element.5), kind=kOutput, calls=%fused_computation.6 | convolution fusion | flops 270532608 | bytes 10617600 | tf_op jit(solution)/shard_map/nrkj,rkij->rni/dot_general | solution.py:48
  55.4 0.1 fusion.18
  55.5 0.1 reshape.139
  55.6 0.1 reshape.116
  55.8 6.6 %fusion.15 = f32[8,32,32,128]{3,1,2,0:T(8,128)} fusion(bf16[8,32,128,128]{3,2,1,0:T(8,128)(2,1)} %param.9, bf16[8,32,128,1]{2,0,1,3:T(8,128)(2,1)S(1)} %bitcast.49), kind=kOutput, calls=%fused_computation.21 | convolution fusion | flops 268435456 | bytes 12648448 | tf_op jit(solution)/shard_map/rni,rkij->nrkj/dot_general | solution.py:67
  62.4 0.1 broadcast_in_dim.16
  62.5 22.6 %scatter_fusion = f32[32,64,128]{2,0,1:T(8,128)S(1)} fusion(f32[32,64,128]{2,0,1:T(8,128)S(1)} %broadcast_in_dim.16, s32[256]{0:T(256)S(1)} %bitcast.51, f32[256,32,128]{2,1,0:T(8,128)} %bitcast.45), kind=kCustom, calls=%fused_computation.1 | custom fusion | flops 1048576 | bytes 12583936 | tf_op jit(solution)/shard_map/scatter-add | solution.py:72
  85.1 0.8 copy_bitcast_fusion
  86.0 0.0 reduce-scatter.2.cloned.1.call-update
  86.0 63.3 %reduce-scatter.2.cloned.1.call-done = bf16[32,1024]{1,0:T(8,128)(2,1)} async-done(((bf16[32,8192]{1,0:T(8,128)(2,1)}), bf16[32,1024]{1,0:T(8,128)(2,1)}) %reduce-scatter.2.cloned.1.call-update) | async-done | bytes 65552 | tf_op jit(solution)/shard_map/reduce_scatter | solution.py:78
  149.3 0.9 convert_subtract_fusion
  150.2 0.7 all_to_all.32
  150.9 3.6 %all-to-all-start.1 = ((f32[8,4,1024]{2,1,0:T(4,128)}), f32[8,4,1024]{2,1,0:T(4,128)S(1)}, u32[]{:S(2)}, u32[]{:S(2)}) async-start(f32[8,4,1024]{2,1,0:T(4,128)} %all_to_all.32), calls=%async_computation.2 | async-start | bytes 262144 | tf_op jit(solution)/shard_map/all_to_all | solution.py:86
  154.5 7.3 %all-to-all-done.1 = f32[8,4,1024]{2,1,0:T(4,128)S(1)} async-done(((f32[8,4,1024]{2,1,0:T(4,128)}), f32[8,4,1024]{2,1,0:T(4,128)S(1)}, u32[]{:S(2)}, u32[]{:S(2)}) %all-to-all-start.1) | async-done | bytes 131104 | tf_op jit(solution)/shard_map/all_to_all | solution.py:86
  161.9 0.7 fusion.10
  (16 shorter events, 0.2 us)
Async XLA Ops:
  6.5 49.2 %all-to-all-start = ((f32[4,8,1024]{2,0,1:T(4,128)}), f32[4,8,1024]{2,0,1:T(4,128)S(1)}, u32[]{:S(2)}, u32[]{:S(2)}) async-start(f32[4,8,1024]{2,0,1:T(4,128)} %bitcast.50), calls=%async_computation | async-start | bytes 262144 | tf_op jit(solution)/shard_map/all_to_all | solution.py:36
  13.8 135.5 %reduce-scatter.2.cloned.1.call-start = ((), (), s32[]{:S(2)}) async-start(), calls=%async_computation.3 | async-start | bytes 589824 | tf_op jit(solution)/shard_map/reduce_scatter | solution.py:78
  50.2 5.2 %copy-start.2 = (s32[8,32]{1,0:T(8,128)S(1)}, s32[8,32]{1,0:T(8,128)}, u32[]{:S(2)}) copy-start(s32[8,32]{1,0:T(8,128)} %param.10) | copy-start | bytes 3076
  50.2 5.2 %copy-start.3 = (s32[8]{0:T(128)S(1)}, s32[8]{0:T(128)}, u32[]{:S(2)}) copy-start(s32[8]{0:T(128)} %param.11) | copy-start | bytes 100
  62.5 92.0 %copy-start.1 = (f32[8192]{0:T(1024)S(1)}, f32[8192]{0:T(1024)}, u32[]{:S(2)}) copy-start(f32[8192]{0:T(1024)} %param.7) | copy-start | bytes 98308
  62.5 99.3 %copy-start = (f32[4,8192]{1,0:T(4,128)S(1)}, f32[4,8192]{1,0:T(4,128)}, u32[]{:S(2)}) copy-start(f32[4,8192]{1,0:T(4,128)} %param.6) | copy-start | bytes 393220
  150.9 11.0 %all-to-all-start.1 = ((f32[8,4,1024]{2,1,0:T(4,128)}), f32[8,4,1024]{2,1,0:T(4,128)S(1)}, u32[]{:S(2)}, u32[]{:S(2)}) async-start(f32[8,4,1024]{2,1,0:T(4,128)} %all_to_all.32), calls=%async_computation.2 | async-start | bytes 262144 | tf_op jit(solution)/shard_map/all_to_all | solution.py:86
Sparse Core Ops, SparseCore 0:
  86.1 63.1 reduce-scatter.1
where the time goes:
time: 170 us; the launch traced here: 169 us
  waiting for transfers between devices  70.7 us (42%)
  blocking collectives  31.9 us (19%)
  other arithmetic  26.8 us (16%)
  between operations  13.5 us (8%)
  matrix products  11.7 us (7%)
  starting transfers between devices  10.9 us (6%)
  local copies, waits for them, and re-layouts  3.74 us (2%)
    reduce_scatter x1, waiting for transfers between devices, on_device(): lax.psum_scatter(collected.reshape(sample_total, surface_range).astype(jn...  63.3 us
    all_gather x1, blocking collectives, on_device(): panel_rows = lax.all_gather(radiant_output, 'node', axis=0, tiled=True)  31.9 us
    scatter-add x1, other arithmetic, update(): return running.at[:, targets, :].add(contrib, mode='drop')  22.6 us
    all_to_all x1, waiting for transfers between devices, on_device(): lax.all_to_all(summed, 'node', split_axis=0, concat_axis=1, tiled=True)  7.33 us
    all_to_all x1, starting transfers between devices, on_device(): lax.all_to_all(loss_factors, 'node', split_axis=1, concat_axis=0, tiled=T...  7.28 us
    dot_general x1, matrix products, update(): jnp.einsum('rni,rkij->nrkj', weight_part, tiles, preferred_element_type=j...  6.55 us
    dot_general x1, matrix products, update(): jnp.einsum('nrkj,rkij->rni', picked, tiles, preferred_element_type=jnp.fl...  5.19 us
    all_to_all x1, starting transfers between devices, on_device(): lax.all_to_all(summed, 'node', split_axis=0, concat_axis=1, tiled=True)  3.62 us
  transfers between devices with their start and end apart: 3, of which 2 were waited for; matrix products, arithmetic and copies ran while one was open for 6% of the time, Pallas kernels for 0%

commit v1 on v0

--- a/solution.py
+++ b/solution.py
@@ -2,6 +2,27 @@
 import jax.numpy as jnp
 from jax import lax
 from jax.sharding import PartitionSpec as P
+
+
+def collect(value, axis, dim):
+    length, place, rows = (lax.axis_size(axis), lax.axis_index(axis), value.shape[dim])
+    forward = [(i, (i + 1) % length) for i in range(length)]
+    left = [(i, (i - 1) % length) for i in range(length)]
+    out = jnp.zeros((*value.shape[:dim], length * rows, *value.shape[dim + 1 :]), value.dtype)
+    out = lax.dynamic_update_slice_in_dim(out, value, place * rows, axis=dim)
+    from_left = from_right = value
+    half = length // 2
+    for hop in range(1, half + 1):
+        from_left = lax.ppermute(from_left, axis, forward)
+        out = lax.dynamic_update_slice_in_dim(
+            out, from_left, (place - hop) % length * rows, axis=dim
+        )
+        if hop < length - half:
+            from_right = lax.ppermute(from_right, axis, left)
+            out = lax.dynamic_update_slice_in_dim(
+                out, from_right, (place + hop) % length * rows, axis=dim
+            )
+    return out
 
 
 def slot_window(gebhart_tiles, tile_target_index, tile_slots_occupied, slot_start, slot_width):
@@ -34,7 +55,7 @@
     own_start = lax.axis_index("node") * own_width
     radiant_output = (surface_emittance[None, :] * scaled_kelvin**4).astype(jnp.bfloat16)
     weights_here = lax.all_to_all(loss_factors, "node", split_axis=1, concat_axis=0, tiled=True)
-    panel_rows = lax.all_gather(radiant_output, "node", axis=0, tiled=True)
+    panel_rows = collect(radiant_output, "node", 0)
     row_count = panel_rows.shape[0]
     panel_view = panel_rows.reshape(row_count, blocks_all, block_side)
 

time: 170 us -> 158 us (0.929)
  blocking collectives: 31.9 us -> 0 us
  starting transfers between devices: 10.9 us -> 22.6 us
  waiting for transfers between devices: 70.7 us -> 78.3 us
    all_gather x1 -> x0, blocking collectives: 31.9 us -> none  [on_device(): panel_rows = lax.all_gather(radiant_output, 'node', axis=0, tiled=True)]
    ppermute x0 -> x7, starting transfers between devices: none -> 15.6 us  [the longest x3 10.8 us: collect(): from_right = lax.ppermute(from_right, axis, left)]
    ppermute x0 -> x7, waiting for transfers between devices: none -> 11 us  [the longest x4 11 us: collect(): from_left = lax.ppermute(from_left, axis, forward)]
    all_to_all x1, starting transfers between devices: 7.28 us -> 3.37 us  [on_device(): lax.all_to_all(loss_factors, 'node', split_axis=1, concat_axis=0, tiled=T...]
    reduce_scatter x1, waiting for transfers between devices: 63.3 us -> 59.9 us  [on_device(): lax.psum_scatter(collected.reshape(sample_total, surface_range).astype(jn...]
  transfers between devices with their start and end apart: 3 -> 10, of which waited for: 2 -> 5; matrix products, arithmetic and copies ran while one was open for 6% -> 2% of each run, Pallas kernels for 0% -> 0%
where the time goes in v1:
time: 158 us; the launch traced here: 157 us
  waiting for transfers between devices  78.3 us (50%)
  other arithmetic  27.6 us (17%)
  starting transfers between devices  22.6 us (14%)
  between operations  13.7 us (9%)
  matrix products  11.7 us (7%)
  local copies, waits for them, and re-layouts  3.19 us (2%)
    reduce_scatter x1, waiting for transfers between devices, on_device(): lax.psum_scatter(collected.reshape(sample_total, surface_range).astype(jn...  59.9 us
    scatter-add x1, other arithmetic, update(): return running.at[:, targets, :].add(contrib, mode='drop')  22.6 us
    ppermute x4, waiting for transfers between devices, collect(): from_left = lax.ppermute(from_left, axis, forward)  11 us
    ppermute x3, starting transfers between devices, collect(): from_right = lax.ppermute(from_right, axis, left)  10.8 us
    all_to_all x1, waiting for transfers between devices, on_device(): lax.all_to_all(summed, 'node', split_axis=0, concat_axis=1, tiled=True)  7.33 us
    dot_general x1, matrix products, update(): jnp.einsum('rni,rkij->nrkj', weight_part, tiles, preferred_element_type=j...  6.56 us
    dot_general x1, matrix products, update(): jnp.einsum('nrkj,rkij->rni', picked, tiles, preferred_element_type=jnp.fl...  5.19 us
    ppermute x4, starting transfers between devices, collect(): from_left = lax.ppermute(from_left, axis, forward)  4.83 us
  transfers between devices with their start and end apart: 10, of which 5 were waited for; matrix products, arithmetic and copies ran while one was open for 2% of the time, Pallas kernels for 0%

profile of v1, /device:TPU:0, one launch (start us, length us, event | category | flops | bytes accessed | tf_op | source)
XLA Modules:
  0.0 157.1 jit_solution(10213907895184045333)
XLA Ops:
  6.6 1.0 constant_dynamic-update-slice_fusion.7
  7.6 3.0 %collective-permute-start = (bf16[4,8192]{1,0:T(4,128)(2,1)S(1)}, bf16[4,8192]{1,0:T(4,128)(2,1)S(1)}, u32[]{:S(2)}, u32[]{:S(2)}) collective-permute-start(bf16[4,8192]{1,0:T(4,128)(2,1)S(1)} %get-tuple-element.6), channel_id=1, source_target_pairs={{0,2},{2,4},{4,6},{6,8},{8,10},{10,12},{12,14},{14,0},{1,3},{3,5},... | collective-permute-start | bytes 196616 | tf_op jit(solution)/shard_map/ppermute | solution.py:16
  10.6 3.1 %collective-permute-start.1 = (bf16[4,8192]{1,0:T(4,128)(2,1)S(1)}, bf16[4,8192]{1,0:T(4,128)(2,1)S(1)}, u32[]{:S(2)}, u32[]{:S(2)}) collective-permute-start(bf16[4,8192]{1,0:T(4,128)(2,1)S(1)} %get-tuple-element.6), channel_id=1, source_target_pairs={{0,14},{2,0},{4,2},{6,4},{8,6},{10,8},{12,10},{14,12},{1,15},{3,1}... | collective-permute-start | bytes 196616 | tf_op jit(solution)/shard_map/ppermute | solution.py:21
  13.7 3.4 %all-to-all-start = ((f32[4,8,1024]{2,0,1:T(4,128)}), f32[4,8,1024]{2,0,1:T(4,128)S(1)}, u32[]{:S(2)}, u32[]{:S(2)}) async-start(f32[4,8,1024]{2,0,1:T(4,128)} %bitcast.53), calls=%async_computation | async-start | bytes 262144 | tf_op jit(solution)/shard_map/all_to_all | solution.py:57
  17.2 0.8 reshape.118
  18.0 0.8 fusion.17
  18.8 0.8 fusion.16
  19.6 1.8 %collective-permute-start.2 = (bf16[4,8192]{1,0:T(4,128)(2,1)S(1)}, bf16[4,8192]{1,0:T(4,128)(2,1)S(1)}, u32[]{:S(2)}, u32[]{:S(2)}) collective-permute-start(bf16[4,8192]{1,0:T(4,128)(2,1)S(1)} %collective-permute-done), channel_id=1, source_target_pairs={{0,2},{2,4},{4,6},{6,8},{8,10},{10,12},{12,14},{14,0},{1,3},{3,5},... | collective-permute-start | bytes 196616 | tf_op jit(solution)/shard_map/ppermute | solution.py:16
  21.4 3.0 %collective-permute-start.3 = (bf16[4,8192]{1,0:T(4,128)(2,1)S(1)}, bf16[4,8192]{1,0:T(4,128)(2,1)S(1)}, u32[]{:S(2)}, u32[]{:S(2)}) collective-permute-start(bf16[4,8192]{1,0:T(4,128)(2,1)S(1)} %collective-permute-done.1), channel_id=1, source_target_pairs={{0,14},{2,0},{4,2},{6,4},{8,6},{10,8},{12,10},{14,12},{1,15},{3,1}... | collective-permute-start | bytes 196616 | tf_op jit(solution)/shard_map/ppermute | solution.py:21
  24.5 2.1 %collective-permute-done.2 = bf16[4,8192]{1,0:T(4,128)(2,1)S(1)} collective-permute-done((bf16[4,8192]{1,0:T(4,128)(2,1)S(1)}, bf16[4,8192]{1,0:T(4,128)(2,1)S(1)}, u32[]{:S(2)}, u32[]{:S(2)}) %collective-permute-start.2) | collective-permute-done | bytes 65568 | tf_op jit(solution)/shard_map/ppermute | solution.py:16
  26.7 4.7 %collective-permute-start.5 = (bf16[4,8192]{1,0:T(4,128)(2,1)S(1)}, bf16[4,8192]{1,0:T(4,128)(2,1)S(1)}, u32[]{:S(2)}, u32[]{:S(2)}) collective-permute-start(bf16[4,8192]{1,0:T(4,128)(2,1)S(1)} %collective-permute-done.3), channel_id=1, source_target_pairs={{0,14},{2,0},{4,2},{6,4},{8,6},{10,8},{12,10},{14,12},{1,15},{3,1}... | collective-permute-start | bytes 196616 | tf_op jit(solution)/shard_map/ppermute | solution.py:21
  31.5 2.1 %collective-permute-done.4 = bf16[4,8192]{1,0:T(4,128)(2,1)S(1)} collective-permute-done((bf16[4,8192]{1,0:T(4,128)(2,1)S(1)}, bf16[4,8192]{1,0:T(4,128)(2,1)S(1)}, u32[]{:S(2)}, u32[]{:S(2)}) %collective-permute-start.4) | collective-permute-done | bytes 65568 | tf_op jit(solution)/shard_map/ppermute | solution.py:16
  33.8 6.8 %collective-permute-done.6 = bf16[4,8192]{1,0:T(4,128)(2,1)S(1)} collective-permute-done((bf16[4,8192]{1,0:T(4,128)(2,1)S(1)}, bf16[4,8192]{1,0:T(4,128)(2,1)S(1)}, u32[]{:S(2)}, u32[]{:S(2)}) %collective-permute-start.6) | collective-permute-done | bytes 65568 | tf_op jit(solution)/shard_map/ppermute | solution.py:16
  40.7 1.0 gather_fusion
  41.7 5.2 %fusion.4 = f32[8,4,8,128]{3,2,1,0:T(8,128)S(1)} fusion(bf16[8,32,128,128]{3,2,1,0:T(8,128)(2,1)} %param.9, bf16[32,8,32,128]{3,0,2,1:T(8,128)(2,1)S(1)} %bitcast.49, pred[8,32]{1,0:T(8,128)(4,1)S(1)} %get-tuple-element.10, bf16[8,32]{1,0:T(8,128)(2,1)S(1)} %get-tuple-element.9), kind=kOutput, calls=%fused_computation.6 | convolution fusion | flops 270532608 | bytes 10617600 | tf_op jit(solution)/shard_map/nrkj,rkij->rni/dot_general | solution.py:69
  47.0 6.6 %fusion.14 = f32[8,32,32,128]{3,1,2,0:T(8,128)} fusion(bf16[8,32,128,128]{3,2,1,0:T(8,128)(2,1)} %param.9, bf16[8,32,128,1]{2,0,1,3:T(8,128)(2,1)S(1)} %bitcast.52), kind=kOutput, calls=%fused_computation.21 | convolution fusion | flops 268435456 | bytes 12648448 | tf_op jit(solution)/shard_map/rni,rkij->nrkj/dot_general | solution.py:88
  53.7 22.6 %scatter_fusion = f32[32,64,128]{2,0,1:T(8,128)S(1)} fusion(f32[32,64,128]{2,0,1:T(8,128)S(1)} %broadcast_in_dim.28, s32[256]{0:T(256)S(1)} %bitcast.54, f32[256,32,128]{2,1,0:T(8,128)} %bitcast.48), kind=kCustom, calls=%fused_computation.1 | custom fusion | flops 1048576 | bytes 12583936 | tf_op jit(solution)/shard_map/scatter-add | solution.py:93
  76.3 0.8 copy_bitcast_fusion
  77.2 59.9 %reduce-scatter.2.cloned.1.call-done = bf16[32,1024]{1,0:T(8,128)(2,1)} async-done(((bf16[32,8192]{1,0:T(8,128)(2,1)}), bf16[32,1024]{1,0:T(8,128)(2,1)}) %reduce-scatter.2.cloned.1.call-update) | async-done | bytes 65552 | tf_op jit(solution)/shard_map/reduce_scatter | solution.py:99
  137.1 0.9 convert_subtract_fusion
  137.9 0.7 all_to_all.32
  138.6 3.6 %all-to-all-start.1 = ((f32[8,4,1024]{2,1,0:T(4,128)}), f32[8,4,1024]{2,1,0:T(4,128)S(1)}, u32[]{:S(2)}, u32[]{:S(2)}) async-start(f32[8,4,1024]{2,1,0:T(4,128)} %all_to_all.32), calls=%async_computation.2 | async-start | bytes 262144 | tf_op jit(solution)/shard_map/all_to_all | solution.py:107
  142.2 7.3 %all-to-all-done.1 = f32[8,4,1024]{2,1,0:T(4,128)S(1)} async-done(((f32[8,4,1024]{2,1,0:T(4,128)}), f32[8,4,1024]{2,1,0:T(4,128)S(1)}, u32[]{:S(2)}, u32[]{:S(2)}) %all-to-all-start.1) | async-done | bytes 131104 | tf_op jit(solution)/shard_map/all_to_all | solution.py:107
  149.6 0.7 fusion.10
  (30 shorter events, 0.9 us)
Async XLA Ops:
  7.6 12.1 %collective-permute-start = (bf16[4,8192]{1,0:T(4,128)(2,1)S(1)}, bf16[4,8192]{1,0:T(4,128)(2,1)S(1)}, u32[]{:S(2)}, u32[]{:S(2)}) collective-permute-start(bf16[4,8192]{1,0:T(4,128)(2,1)S(1)} %get-tuple-element.6), channel_id=1, source_target_pairs={{0,2},{2,4},{4,6},{6,8},{8,10},{10,12},{12,14},{14,0},{1,3},{3,5},... | collective-permute-start | bytes 196616 | tf_op jit(solution)/shard_map/ppermute | solution.py:16
  10.6 10.9 %collective-permute-start.1 = (bf16[4,8192]{1,0:T(4,128)(2,1)S(1)}, bf16[4,8192]{1,0:T(4,128)(2,1)S(1)}, u32[]{:S(2)}, u32[]{:S(2)}) collective-permute-start(bf16[4,8192]{1,0:T(4,128)(2,1)S(1)} %get-tuple-element.6), channel_id=1, source_target_pairs={{0,14},{2,0},{4,2},{6,4},{8,6},{10,8},{12,10},{14,12},{1,15},{3,1}... | collective-permute-start | bytes 196616 | tf_op jit(solution)/shard_map/ppermute | solution.py:21
  13.7 20.1 %all-to-all-start = ((f32[4,8,1024]{2,0,1:T(4,128)}), f32[4,8,1024]{2,0,1:T(4,128)S(1)}, u32[]{:S(2)}, u32[]{:S(2)}) async-start(f32[4,8,1024]{2,0,1:T(4,128)} %bitcast.53), calls=%async_computation | async-start | bytes 262144 | tf_op jit(solution)/shard_map/all_to_all | solution.py:57
  17.1 120.0 %reduce-scatter.2.cloned.1.call-start = ((), (), s32[]{:S(2)}) async-start(), calls=%async_computation.3 | async-start | bytes 589824 | tf_op jit(solution)/shard_map/reduce_scatter | solution.py:99
  19.6 7.0 %collective-permute-start.2 = (bf16[4,8192]{1,0:T(4,128)(2,1)S(1)}, bf16[4,8192]{1,0:T(4,128)(2,1)S(1)}, u32[]{:S(2)}, u32[]{:S(2)}) collective-permute-start(bf16[4,8192]{1,0:T(4,128)(2,1)S(1)} %collective-permute-done), channel_id=1, source_target_pairs={{0,2},{2,4},{4,6},{6,8},{8,10},{10,12},{12,14},{14,0},{1,3},{3,5},... | collective-permute-start | bytes 196616 | tf_op jit(solution)/shard_map/ppermute | solution.py:16
  21.4 5.2 %collective-permute-start.3 = (bf16[4,8192]{1,0:T(4,128)(2,1)S(1)}, bf16[4,8192]{1,0:T(4,128)(2,1)S(1)}, u32[]{:S(2)}, u32[]{:S(2)}) collective-permute-start(bf16[4,8192]{1,0:T(4,128)(2,1)S(1)} %collective-permute-done.1), channel_id=1, source_target_pairs={{0,14},{2,0},{4,2},{6,4},{8,6},{10,8},{12,10},{14,12},{1,15},{3,1}... | collective-permute-start | bytes 196616 | tf_op jit(solution)/shard_map/ppermute | solution.py:21
  26.7 7.0 %collective-permute-start.4 = (bf16[4,8192]{1,0:T(4,128)(2,1)S(1)}, bf16[4,8192]{1,0:T(4,128)(2,1)S(1)}, u32[]{:S(2)}, u32[]{:S(2)}) collective-permute-start(bf16[4,8192]{1,0:T(4,128)(2,1)S(1)} %collective-permute-done.2), channel_id=1, source_target_pairs={{0,2},{2,4},{4,6},{6,8},{8,10},{10,12},{12,14},{14,0},{1,3},{3,5},... | collective-permute-start | bytes 196616 | tf_op jit(solution)/shard_map/ppermute | solution.py:16
  26.7 7.0 %collective-permute-start.5 = (bf16[4,8192]{1,0:T(4,128)(2,1)S(1)}, bf16[4,8192]{1,0:T(4,128)(2,1)S(1)}, u32[]{:S(2)}, u32[]{:S(2)}) collective-permute-start(bf16[4,8192]{1,0:T(4,128)(2,1)S(1)} %collective-permute-done.3), channel_id=1, source_target_pairs={{0,14},{2,0},{4,2},{6,4},{8,6},{10,8},{12,10},{14,12},{1,15},{3,1}... | collective-permute-start | bytes 196616 | tf_op jit(solution)/shard_map/ppermute | solution.py:21
  33.6 7.0 %collective-permute-start.6 = (bf16[4,8192]{1,0:T(4,128)(2,1)S(1)}, bf16[4,8192]{1,0:T(4,128)(2,1)S(1)}, u32[]{:S(2)}, u32[]{:S(2)}) collective-permute-start(bf16[4,8192]{1,0:T(4,128)(2,1)S(1)} %collective-permute-done.4), channel_id=1, source_target_pairs={{0,2},{2,4},{4,6},{6,8},{8,10},{10,12},{12,14},{14,0},{1,3},{3,5},... | collective-permute-start | bytes 196616 | tf_op jit(solution)/shard_map/ppermute | solution.py:16
  53.7 88.5 %copy-start.1 = (f32[8192]{0:T(1024)S(1)}, f32[8192]{0:T(1024)}, u32[]{:S(2)}) copy-start(f32[8192]{0:T(1024)} %param.7) | copy-start | bytes 98308
  53.7 95.9 %copy-start = (f32[4,8192]{1,0:T(4,128)S(1)}, f32[4,8192]{1,0:T(4,128)}, u32[]{:S(2)}) copy-start(f32[4,8192]{1,0:T(4,128)} %param.6) | copy-start | bytes 393220
  138.6 10.9 %all-to-all-start.1 = ((f32[8,4,1024]{2,1,0:T(4,128)}), f32[8,4,1024]{2,1,0:T(4,128)S(1)}, u32[]{:S(2)}, u32[]{:S(2)}) async-start(f32[8,4,1024]{2,1,0:T(4,128)} %all_to_all.32), calls=%async_computation.2 | async-start | bytes 262144 | tf_op jit(solution)/shard_map/all_to_all | solution.py:107
Sparse Core Ops, SparseCore 0:
  77.3 59.7 reduce-scatter.1
